TPU v7x, 128 devices: a whole 4x4x4 slice. The times are simulated.
128 devices in a mesh: row: 8 (over y, core), col: 16 (over x, z).
Axes of the slice: x: 4, y: 4, z: 4, core: 2. Of those that a mesh axis runs over, the one named last changes fastest.
Arguments:
- tokens: bfloat16 [104, 320, 384], P('row', 'col')
- row_sizes: int32 [8], replicated, may hold values from 1 to 13, 88 in all
- col_sizes: int32 [16], replicated, may hold values from 1 to 20, 256 in all
- norm_gain: float32 [384], replicated, may hold values from 0.25 to 1.75
- query_weight: bfloat16 [384, 384], replicated
- key_weight: bfloat16 [384, 384], replicated
- value_weight: bfloat16 [384, 384], replicated, may hold values from -0.3125 to 0.3125
- out_weight: bfloat16 [384, 384], replicated, may hold values from -0.625 to 0.625
- cache_one: bfloat16 [2, 104, 320, 384], P(None, 'row', 'col'), may hold values from -6 to 6
- gain_one: float32 [384], replicated, may hold values from 0.25 to 1.75
- conv_one: bfloat16 [3, 3, 3, 384, 384], replicated, may hold values from -0.0625 to 0.0625
- cache_two: bfloat16 [2, 208, 640, 384], P(None, 'row', 'col'), may hold values from -6 to 6
- gain_two: float32 [384], replicated, may hold values from 0.25 to 1.75
- conv_two: bfloat16 [3, 3, 3, 384, 192], replicated, may hold values from -0.0625 to 0.0625
Outputs:
- decoded: bfloat16 [208, 640, 192], P('row', 'col')
Inputs may be any that keep to these rules, and one draw needn't show every extreme that they name: `row_sizes`: positive tile heights that sum to 88; the tallest has exactly 13 rows. `col_sizes`: positive tile widths that sum to 256; the widest has exactly 20 columns.
All inputs are finite; a program needn't handle non-finite values.
Results may differ from a plain program's by a relative error of at most 0.0095.
Values may be sent and summed in bfloat16 or wider, within the bound.
No kernel may reach another device: no remote copies, remote signals or barrier semaphores. Data moves between devices by JAX's collectives and lax.ppermute only.
A program may use at most 320 MiB of HBM per device.

v0:
```python
import math
import jax
import jax.numpy as jnp
from jax import lax
from jax.sharding import PartitionSpec as P

epsilon = 1e-06
masked_score = -1e30


def with_halo(block, sides, width):
    for axis, dim in sides:
        count = lax.axis_size(axis)
        forward = [(i, i + 1) for i in range(count - 1)]
        backward = [(target, source) for source, target in forward]
        low = lax.ppermute(
            lax.slice_in_dim(block, block.shape[dim] - width, None, axis=dim), axis, forward
        )
        high = lax.ppermute(lax.slice_in_dim(block, 0, width, axis=dim), axis, backward)
        block = jnp.concatenate([low, block, high], axis=dim)
    return block


def select_size(size_table, position):
    marks = jnp.arange(size_table.shape[0], dtype=jnp.int32) == position
    return jnp.sum(jnp.where(marks, size_table, 0))


def lookup(size_table, positions):
    marks = positions[:, None] == jnp.arange(size_table.shape[0], dtype=jnp.int32)[None, :]
    return jnp.sum(jnp.where(marks, size_table[None, :], 0), axis=1)


def rms_scale(values_in, gain_vec):
    wide = values_in.astype(jnp.float32)
    return wide * lax.rsqrt(jnp.mean(wide * wide, axis=-1, keepdims=True) + epsilon) * gain_vec


def edge_rows(frames, row_count, col_count):
    height = frames.shape[1]
    breadth = frames.shape[2]
    last_row = lax.dynamic_slice_in_dim(frames, row_count - 1, 1, 1)
    frames = lax.dynamic_update_slice_in_dim(frames, last_row, height - 1, 1)
    last_col = lax.dynamic_slice_in_dim(frames, col_count - 1, 1, 2)
    return lax.dynamic_update_slice_in_dim(frames, last_col, breadth - 1, 2)


def settle(padded, row_count, col_count):
    bottom = padded[:, -1:]
    padded = lax.dynamic_update_slice_in_dim(padded, bottom, row_count + 1, 1)
    right_col = padded[:, :, -1:]
    return lax.dynamic_update_slice_in_dim(padded, right_col, col_count + 1, 2)


def convolve(extended, kernel):
    channels = extended.shape[3]
    height = extended.shape[1] - 2
    breadth = extended.shape[2] - 2
    columns = [
        extended[t_step, a_step : a_step + height, b_step : b_step + breadth]
        for t_step in range(3)
        for a_step in range(3)
        for b_step in range(3)
    ]
    stacked = jnp.concatenate(columns, axis=-1).reshape(height * breadth, 27 * channels)
    product = jnp.dot(
        stacked, kernel.reshape(27 * channels, kernel.shape[-1]), preferred_element_type=jnp.float32
    )
    return product.reshape(height, breadth, kernel.shape[-1])


def upsample(frames):
    return jnp.repeat(jnp.repeat(frames, 2, axis=1), 2, axis=2)


def local(
    tokens,
    row_sizes,
    col_sizes,
    norm_gain,
    query_weight,
    key_weight,
    value_weight,
    out_weight,
    cache_one,
    gain_one,
    conv_one,
    cache_two,
    gain_two,
    conv_two,
):
    tile_rows, tile_cols, channels = tokens.shape
    col_devices = lax.axis_size("col")
    row_count = select_size(row_sizes, lax.axis_index("row"))
    col_count = select_size(col_sizes, lax.axis_index("col"))
    per_device = tile_rows * tile_cols
    scale = 1.0 / math.sqrt(channels)
    flat_normed = rms_scale(tokens, norm_gain).astype(jnp.bfloat16).reshape(per_device, channels)
    queries = jnp.dot(flat_normed, query_weight, preferred_element_type=jnp.float32).astype(
        jnp.bfloat16
    )
    own_keys = jnp.dot(flat_normed, key_weight, preferred_element_type=jnp.float32).astype(
        jnp.bfloat16
    )
    own_values = jnp.dot(flat_normed, value_weight, preferred_element_type=jnp.float32).astype(
        jnp.bfloat16
    )
    key_rows = lax.all_gather(own_keys, ("row", "col"), axis=0, tiled=True)
    running_max = jnp.full((per_device,), masked_score, jnp.float32)
    slot_index = jnp.arange(key_rows.shape[0], dtype=jnp.int32)
    device = slot_index // per_device
    local_slot = slot_index - device * per_device
    tile_row = device // col_devices
    tile_col = device - tile_row * col_devices
    local_row = local_slot // tile_cols
    local_col = local_slot - local_row * tile_cols
    usable = (local_row < lookup(row_sizes, tile_row)) & (local_col < lookup(col_sizes, tile_col))
    scores = jnp.einsum("qc,kc->qk", queries, key_rows, preferred_element_type=jnp.float32) * scale
    scores = jnp.where(usable[None, :], scores, masked_score)
    new_max = jnp.maximum(running_max, jnp.max(scores, axis=1))
    expos = jnp.exp(scores - new_max[:, None]) * usable[None, :].astype(jnp.float32)
    denominator = jnp.sum(expos, axis=1)
    accumulated = jnp.dot(
        expos.astype(jnp.bfloat16),
        lax.all_gather(own_values, ("row", "col"), axis=0, tiled=True),
        preferred_element_type=jnp.float32,
    )
    attention = (accumulated / denominator[:, None]).astype(jnp.bfloat16)
    projected = jnp.dot(attention, out_weight, preferred_element_type=jnp.float32).reshape(
        tile_rows, tile_cols, channels
    )
    mixed = (tokens.astype(jnp.float32) + projected).astype(jnp.bfloat16)
    act_one = jax.nn.silu(rms_scale(mixed, gain_one)).astype(jnp.bfloat16)
    frames_one = jnp.concatenate([cache_one, act_one[None]], axis=0)
    prepared = edge_rows(frames_one, row_count, col_count)
    padded = with_halo(prepared, (("row", 1), ("col", 2)), 1)
    extended = settle(padded, row_count, col_count)
    y_one = convolve(extended, conv_one).astype(jnp.bfloat16)
    act_small = jax.nn.silu(rms_scale(y_one, gain_two)).astype(jnp.bfloat16)[None]
    fine_rows = 2 * row_count
    fine_cols = 2 * col_count
    frames_two = jnp.concatenate([cache_two, upsample(act_small)], axis=0)
    prepared_two = edge_rows(frames_two, fine_rows, fine_cols)
    padded_two = with_halo(prepared_two, (("row", 1), ("col", 2)), 1)
    extended_two = settle(padded_two, fine_rows, fine_cols)
    y_two = convolve(extended_two, conv_two)
    row_usable = jnp.arange(2 * tile_rows, dtype=jnp.int32) < fine_rows
    col_usable = jnp.arange(2 * tile_cols, dtype=jnp.int32) < fine_cols
    usable = (row_usable[:, None] & col_usable[None, :])[:, :, None]
    return jnp.where(usable, y_two, 0.0).astype(jnp.bfloat16)


def solution(mesh):
    placed = (
        P("row", "col", None),
        P(),
        P(),
        P(),
        P(),
        P(),
        P(),
        P(),
        P(None, "row", "col", None),
        P(),
        P(),
        P(None, "row", "col", None),
        P(),
        P(),
    )
    return jax.shard_map(
        local, mesh=mesh, in_specs=placed, out_specs=P("row", "col", None), check_vma=False
    )
```

profile of v0, /device:TPU:3, one launch (start us, length us, event | category | flops | bytes accessed | tf_op | source)
XLA Modules:
  0.0 391.6 jit_solution(13467160023956242634)
XLA Ops:
  8.8 1.9 fusion.15
  10.8 1.9 fusion.16
  13.9 1.4 fusion.93
  16.6 1.3 fusion.94
  21.8 86.2 %all-gather.5.cloned.1.call-done = bf16[128,260,384]{2,1,0:T(8,128)(2,1)} async-done(((bf16[1,260,384]{2,1,0:T(8,128)(2,1)}), bf16[128,260,384]{2,1,0:T(8,128)(2,1)}) %all-gather.5.cloned.1.call-update) | async-done | bytes 25559056 | tf_op jit(solution)/shard_map/all_gather | solution.py:108
  108.0 31.3 %reshape.388 = bf16[33280,384]{1,0:T(8,128)(2,1)} reshape(bf16[128,260,384]{2,1,0:T(8,128)(2,1)} %all-gather.5.cloned.1.call-done) | data formatting | bytes 51118080
  139.3 25.2 %fusion.99 = (f32[260]{0:T(512)S(1)}, f32[260,33280]{1,0:T(8,128)}) fusion(bf16[33280,384]{1,0:T(8,128)(2,1)} %reshape.388, bf16[260,384]{1,0:T(8,128)(2,1)S(1)} %reshape.383, bf16[384,384]{1,0:T(8,128)(2,1)S(1)} %copy-done, pred[33280]{0:T(1024)(128)(4,1)S(1)} %get-tuple-element.6), kind=kOutput, calls=%fused_computation.208 | convolution fusion | flops 6748085248 | bytes 60699152 | tf_op jit(solution)/shard_map/qc,kc->qk/dot_general | solution.py:118
  164.5 17.4 %fusion.1 = f32[260]{0:T(512)S(1)} fusion(f32[260,33280]{1,0:T(8,128)} %get-tuple-element.16, f32[33280]{0:T(1024)S(1)} %get-tuple-element.5, f32[260]{0:T(512)S(1)} %broadcast_maximum_fusion), kind=kLoop, calls=%fused_computation.3 | loop fusion | flops 25958140 | bytes 34746400 | tf_op jit(solution)/shard_map/reduce_sum | solution.py:122
  181.9 22.9 %all-gather.7.cloned.1.call-done = bf16[128,260,384]{2,1,0:T(8,128)(2,1)} async-done(((bf16[1,260,384]{2,1,0:T(8,128)(2,1)}), bf16[128,260,384]{2,1,0:T(8,128)(2,1)}) %all-gather.7.cloned.1.call-update) | async-done | bytes 25559056 | tf_op jit(solution)/shard_map/all_gather | solution.py:125
  204.8 31.2 %reshape.390 = bf16[33280,384]{1,0:T(8,128)(2,1)} reshape(bf16[128,260,384]{2,1,0:T(8,128)(2,1)} %all-gather.7.cloned.1.call-done) | data formatting | bytes 51118080
  236.0 22.0 %fusion.12 = bf16[260,384]{1,0:T(8,128)(2,1)S(1)} fusion(bf16[33280,384]{1,0:T(8,128)(2,1)} %reshape.390, f32[260,33280]{1,0:T(8,128)} %get-tuple-element.16, f32[33280]{0:T(1024)S(1)} %get-tuple-element.5, f32[260]{0:T(512)S(1)} %broadcast_maximum_fusion, f32[260]{0:T(512)S(1)} %fusion.1), kind=kOutput, calls=%fused_computation.19 | convolution fusion | flops 6671508480 | bytes 60505120 | tf_op jit(solution)/shard_map/dot_general | solution.py:123
  259.0 1.5 dynamic_update_slice.25
  260.6 3.3 collective-permute-start
  263.9 1.9 collective-permute-start.1
  265.8 1.6 constant_dynamic-update-slice_fusion.1
  269.5 1.9 collective-permute-start.2
  271.4 5.7 %collective-permute-start.3 = (bf16[3,15,1,384]{3,2,1,0:T(2,128)(2,1)S(1)}, bf16[3,15,1,384]{3,2,1,0:T(2,128)(2,1)}, u32[]{:S(2)}, u32[]{:S(2)}) collective-permute-start(bf16[3,15,1,384]{3,2,1,0:T(2,128)(2,1)S(1)} %get-tuple-element.12), channel_id=1, source_target_pairs={{1,0},{2,1},{3,2},{4,3},{5,4},{6,5},{7,6},{8,7},{9,8},{10,9},{11,1... | collective-permute-start | bytes 103688 | tf_op jit(solution)/shard_map/ppermute | solution.py:19
  280.2 1.7 pad_maximum_fusion.2
  282.0 1.8 dynamic_update_slice.27
  285.7 6.2 %multiply_reduce_fusion = (f32[13,20]{1,0:T(8,128)S(1)}, f32[13,20,384]{2,1,0:T(8,128)S(1)}) fusion(bf16[13,20,10368]{2,1,0:T(8,128)(2,1)S(1)} %fusion.57, bf16[10368,384,1]{1,0,2:T(8,128)(2,1)} %bitcast.243), kind=kOutput, calls=%fused_computation.100 | convolution fusion | flops 2070681344 | bytes 13754384 | tf_op jit(solution)/shard_map/dot_general | solution.py:66
  295.2 3.4 dynamic_update_slice.29
  298.7 3.0 collective-permute-start.4
  301.7 1.9 collective-permute-start.5
  303.6 3.9 %collective-permute-done.5 = bf16[3,1,40,384]{3,2,1,0:T(8,128)(2,1)S(1)} collective-permute-done((bf16[3,1,40,384]{3,2,1,0:T(8,128)(2,1)S(1)}, bf16[3,1,40,384]{3,2,1,0:T(8,128)(2,1)S(1)}, u32[]{:S(2)}, u32[]{:S(2)}) %collective-permute-start.5) | collective-permute-done | bytes 92192 | tf_op jit(solution)/shard_map/ppermute | solution.py:19
  307.7 1.9 collective-permute-start.6
  309.7 5.5 %collective-permute-start.7 = (bf16[3,28,1,384]{3,2,1,0:T(2,128)(2,1)S(1)}, bf16[3,28,1,384]{3,2,1,0:T(2,128)(2,1)}, u32[]{:S(2)}, u32[]{:S(2)}) collective-permute-start(bf16[3,28,1,384]{3,2,1,0:T(2,128)(2,1)S(1)} %get-tuple-element.8), channel_id=1, source_target_pairs={{1,0},{2,1},{3,2},{4,3},{5,4},{6,5},{7,6},{8,7},{9,8},{10,9},{11,1... | collective-permute-start | bytes 193544 | tf_op jit(solution)/shard_map/ppermute | solution.py:19
  315.2 7.9 %copy.21 = bf16[3,3,3,384,192]{3,2,1,0,4:T(4,128)(2,1)} copy(bf16[3,3,3,384,192]{3,4,2,1,0:T(8,128)(2,1)} %param.27) | data formatting | bytes 7962624 | tf_op args[13]
  323.1 10.1 %reshape.392 = bf16[10368,192,1]{0,1,2:T(8,128)(2,1)} reshape(bf16[3,3,3,384,192]{3,2,1,0,4:T(4,128)(2,1)} %copy.21) | data formatting | bytes 7962624 | tf_op jit(solution)/shard_map/reshape | solution.py:67
  333.9 4.4 %pad_maximum_fusion = bf16[3,28,42,384]{3,2,1,0:T(8,128)(2,1)S(1)} fusion(bf16[3,28,1,384]{3,2,1,0:T(2,128)(2,1)} %collective-permute-done.7, bf16[3,1,40,384]{3,2,1,0:T(8,128)(2,1)S(1)} %collective-permute-done.5, bf16[3,26,40,384]{3,2,1,0:T(8,128)(2,1)} %copy-done.2, bf16[3,1,40,384]{3,2,1,0:T(8,128)(2,1)S(1)} %collective-permute-done.4, ...), kind=kLoop, calls=%fused_computation.8 | loop fusion | flops 13547520 | bytes 5419008 | tf_op jit(solution)/shard_map/concatenate | solution.py:20
  338.5 3.6 dynamic_update_slice.31
  361.7 1.3 fusion.26
  373.6 11.2 %fusion.7 = bf16[26,40,192]{2,1,0:T(8,128)(2,1)} fusion(bf16[26,40,10368]{2,1,0:T(8,128)(2,1)} %fusion.17, bf16[10368,192,1]{0,1,2:T(8,128)(2,1)S(1)} %copy-done.4, pred[26,40]{1,0:T(8,128)(4,1)S(1)} %broadcast_and_fusion), kind=kOutput, calls=%fused_computation.12 | convolution fusion | flops 4140963840 | bytes 25947152 | tf_op jit(solution)/shard_map/dot_general | solution.py:66
  (125 shorter events, 44.9 us)
Async XLA Ops:
  6.5 132.8 %copy-start = (bf16[384,384]{1,0:T(8,128)(2,1)S(1)}, bf16[384,384]{1,0:T(8,128)(2,1)}, u32[]{:S(2)}) copy-start(bf16[384,384]{1,0:T(8,128)(2,1)} %param.18) | copy-start | bytes 884740
  6.5 101.5 %all-gather.5.cloned.1.call-start = ((), (), s32[]{:S(2)}) async-start(), calls=%async_computation | async-start | bytes 26155008 | tf_op jit(solution)/shard_map/all_gather | solution.py:108
  10.8 194.0 %all-gather.7.cloned.1.call-start = ((), (), s32[]{:S(2)}) async-start(), calls=%async_computation.1 | async-start | bytes 26155008 | tf_op jit(solution)/shard_map/all_gather | solution.py:125
  236.0 22.0 %copy-start.6 = (bf16[384,384]{1,0:T(8,128)(2,1)S(1)}, bf16[384,384]{1,0:T(8,128)(2,1)}, u32[]{:S(2)}) copy-start(bf16[384,384]{1,0:T(8,128)(2,1)} %param.21) | copy-start | bytes 884740
  236.0 22.4 %copy-start.5 = (bf16[13,20,384]{2,1,0:T(8,128)(2,1)S(1)}, bf16[13,20,384]{2,1,0:T(8,128)(2,1)}, u32[]{:S(2)}) copy-start(bf16[13,20,384]{2,1,0:T(8,128)(2,1)} %param.14) | copy-start | bytes 599044
  236.0 22.5 %copy-start.8 = (f32[384]{0:T(512)S(1)}, f32[384]{0:T(512)}, u32[]{:S(2)}) copy-start(f32[384]{0:T(512)} %param.23) | copy-start | bytes 4612
  260.6 19.6 %copy-start.3 = (bf16[3,13,20,384]{3,2,1,0:T(8,128)(2,1)}, bf16[3,13,20,384]{3,2,1,0:T(8,128)(2,1)S(1)}, u32[]{:S(2)}) copy-start(bf16[3,13,20,384]{3,2,1,0:T(8,128)(2,1)S(1)} %dynamic_update_slice.25) | copy-start | bytes 1797124
  260.6 7.5 %collective-permute-start = (bf16[3,1,20,384]{3,2,1,0:T(8,128)(2,1)S(1)}, bf16[3,1,20,384]{3,2,1,0:T(8,128)(2,1)S(1)}, u32[]{:S(2)}, u32[]{:S(2)}) collective-permute-start(bf16[3,1,20,384]{3,2,1,0:T(8,128)(2,1)S(1)} %get-tuple-element.13), channel_id=1, source_target_pairs={{0,16},{16,32},{32,48},{48,64},{64,80},{80,96},{96,112},{1,17},{17... | collective-permute-start | bytes 138248 | tf_op jit(solution)/shard_map/ppermute | solution.py:16
  263.9 5.5 %collective-permute-start.1 = (bf16[3,1,20,384]{3,2,1,0:T(8,128)(2,1)S(1)}, bf16[3,1,20,384]{3,2,1,0:T(8,128)(2,1)S(1)}, u32[]{:S(2)}, u32[]{:S(2)}) collective-permute-start(bf16[3,1,20,384]{3,2,1,0:T(8,128)(2,1)S(1)} %get-tuple-element.14), channel_id=1, source_target_pairs={{16,0},{32,16},{48,32},{64,48},{80,64},{96,80},{112,96},{17,1},{33... | collective-permute-start | bytes 138248 | tf_op jit(solution)/shard_map/ppermute | solution.py:19
  269.5 10.7 %collective-permute-start.2 = (bf16[3,15,1,384]{3,2,1,0:T(2,128)(2,1)S(1)}, bf16[3,15,1,384]{3,2,1,0:T(2,128)(2,1)S(1)}, u32[]{:S(2)}, u32[]{:S(2)}) collective-permute-start(bf16[3,15,1,384]{3,2,1,0:T(2,128)(2,1)S(1)} %get-tuple-element.11), channel_id=1, source_target_pairs={{0,1},{1,2},{2,3},{3,4},{4,5},{5,6},{6,7},{7,8},{8,9},{9,10},{10,1... | collective-permute-start | bytes 103688 | tf_op jit(solution)/shard_map/ppermute | solution.py:16
  271.4 8.8 %collective-permute-start.3 = (bf16[3,15,1,384]{3,2,1,0:T(2,128)(2,1)S(1)}, bf16[3,15,1,384]{3,2,1,0:T(2,128)(2,1)}, u32[]{:S(2)}, u32[]{:S(2)}) collective-permute-start(bf16[3,15,1,384]{3,2,1,0:T(2,128)(2,1)S(1)} %get-tuple-element.12), channel_id=1, source_target_pairs={{1,0},{2,1},{3,2},{4,3},{5,4},{6,5},{7,6},{8,7},{9,8},{10,9},{11,1... | collective-permute-start | bytes 103688 | tf_op jit(solution)/shard_map/ppermute | solution.py:19
  285.6 6.2 %copy-start.9 = (f32[384]{0:T(512)S(1)}, f32[384]{0:T(512)}, u32[]{:S(2)}) copy-start(f32[384]{0:T(512)} %param.26) | copy-start | bytes 4612
  298.7 34.5 %copy-start.2 = (bf16[3,26,40,384]{3,2,1,0:T(8,128)(2,1)}, bf16[3,26,40,384]{3,2,1,0:T(8,128)(2,1)S(1)}, u32[]{:S(2)}) copy-start(bf16[3,26,40,384]{3,2,1,0:T(8,128)(2,1)S(1)} %dynamic_update_slice.29) | copy-start | bytes 7188484
  298.7 4.9 %collective-permute-start.4 = (bf16[3,1,40,384]{3,2,1,0:T(8,128)(2,1)S(1)}, bf16[3,1,40,384]{3,2,1,0:T(8,128)(2,1)S(1)}, u32[]{:S(2)}, u32[]{:S(2)}) collective-permute-start(bf16[3,1,40,384]{3,2,1,0:T(8,128)(2,1)S(1)} %get-tuple-element.9), channel_id=1, source_target_pairs={{0,16},{16,32},{32,48},{48,64},{64,80},{80,96},{96,112},{1,17},{17... | collective-permute-start | bytes 276488 | tf_op jit(solution)/shard_map/ppermute | solution.py:16
  301.7 5.9 %collective-permute-start.5 = (bf16[3,1,40,384]{3,2,1,0:T(8,128)(2,1)S(1)}, bf16[3,1,40,384]{3,2,1,0:T(8,128)(2,1)S(1)}, u32[]{:S(2)}, u32[]{:S(2)}) collective-permute-start(bf16[3,1,40,384]{3,2,1,0:T(8,128)(2,1)S(1)} %get-tuple-element.10), channel_id=1, source_target_pairs={{16,0},{32,16},{48,32},{64,48},{80,64},{96,80},{112,96},{17,1},{33... | collective-permute-start | bytes 276488 | tf_op jit(solution)/shard_map/ppermute | solution.py:19
  307.7 25.5 %collective-permute-start.6 = (bf16[3,28,1,384]{3,2,1,0:T(2,128)(2,1)S(1)}, bf16[3,28,1,384]{3,2,1,0:T(2,128)(2,1)S(1)}, u32[]{:S(2)}, u32[]{:S(2)}) collective-permute-start(bf16[3,28,1,384]{3,2,1,0:T(2,128)(2,1)S(1)} %get-tuple-element.7), channel_id=1, source_target_pairs={{0,1},{1,2},{2,3},{3,4},{4,5},{5,6},{6,7},{7,8},{8,9},{9,10},{10,1... | collective-permute-start | bytes 193544 | tf_op jit(solution)/shard_map/ppermute | solution.py:16
  309.7 24.2 %collective-permute-start.7 = (bf16[3,28,1,384]{3,2,1,0:T(2,128)(2,1)S(1)}, bf16[3,28,1,384]{3,2,1,0:T(2,128)(2,1)}, u32[]{:S(2)}, u32[]{:S(2)}) collective-permute-start(bf16[3,28,1,384]{3,2,1,0:T(2,128)(2,1)S(1)} %get-tuple-element.8), channel_id=1, source_target_pairs={{1,0},{2,1},{3,2},{4,3},{5,4},{6,5},{7,6},{8,7},{9,8},{10,9},{11,1... | collective-permute-start | bytes 193544 | tf_op jit(solution)/shard_map/ppermute | solution.py:19
  333.2 0.7 copy-start.7
  364.0 9.6 %copy-start.4 = (bf16[10368,192,1]{0,1,2:T(8,128)(2,1)S(1)}, bf16[10368,192,1]{0,1,2:T(8,128)(2,1)}, u32[]{:S(2)}) copy-start(bf16[10368,192,1]{0,1,2:T(8,128)(2,1)} %reshape.392) | copy-start | bytes 11943940
  373.6 11.2 %copy-start.1 = (bf16[384,384]{1,0:T(8,128)(2,1)S(1)}, bf16[384,384]{1,0:T(8,128)(2,1)}, u32[]{:S(2)}) copy-start(bf16[384,384]{1,0:T(8,128)(2,1)} %param.18) | copy-start | bytes 884740
Sparse Core Ops, SparseCore 0:
  10.9 97.1 all-gather.4
  111.0 93.7 all-gather.6
where the time goes:
time: 394 us; the launch traced here: 392 us
  local copies, waits for them, and re-layouts  131 us (33%)
  waiting for transfers between devices  114 us (29%)
  matrix products  68.7 us (17%)
  other arithmetic  32.2 us (8%)
  starting transfers between devices  25.1 us (6%)
  between operations  20.4 us (5%)
    unnamed x77, local copies, waits for them, and re-layouts  106 us
    all_gather x1, waiting for transfers between devices, local(): key_rows = lax.all_gather(own_keys, ('row', 'col'), axis=0, tiled=True)  86.2 us
    dot_general x1, matrix products, local(): jnp.einsum('qc,kc->qk', queries, key_rows, preferred_element_type=jnp.flo...  25.2 us
    all_gather x1, waiting for transfers between devices, local(): lax.all_gather(own_values, ('row', 'col'), axis=0, tiled=True)  22.9 us
    dot_general x1, matrix products, local(): jnp.dot(expos.astype(jnp.bfloat16), lax.all_gather(own_values, ('row', 'c...  22 us
    reduce_sum x1, other arithmetic, local(): denominator = jnp.sum(expos, axis=1)  17.4 us
    dot_general x2, matrix products, convolve(): jnp.dot(stacked, kernel.reshape(27 * channels, kernel.shape[-1]), preferr...  17.3 us
    ppermute x4, starting transfers between devices, with_halo(): lax.ppermute(lax.slice_in_dim(block, 0, width, axis=dim), axis, backward)  15 us
  transfers between devices with their start and end apart: 10, of which 4 were waited for; matrix products, arithmetic and copies ran while one was open for 26% of the time, Pallas kernels for 0%

commit v1 on v0

--- a/solution.py
+++ b/solution.py
@@ -122,7 +122,12 @@
     denominator = jnp.sum(expos, axis=1)
     accumulated = jnp.dot(
         expos.astype(jnp.bfloat16),
-        lax.all_gather(own_values, ("row", "col"), axis=0, tiled=True),
+        jnp.concatenate(
+            lax.all_to_all(
+                jnp.stack([own_values] * lax.axis_size(("row", "col"))), ("row", "col"), 0, 0
+            ),
+            axis=0,
+        ),
         preferred_element_type=jnp.float32,
     )
     attention = (accumulated / denominator[:, None]).astype(jnp.bfloat16)

time: 394 us -> 711 us (1.80)
  waiting for transfers between devices: 114 us -> 395 us
  starting transfers between devices: 25.1 us -> 55.6 us
  local copies, waits for them, and re-layouts: 131 us -> 139 us
    all_to_all x0 -> x1, waiting for transfers between devices: none -> 390 us  [local(): lax.all_to_all(jnp.stack([own_values] * lax.axis_size(('row', 'col'))), (...]
    all_gather x1, waiting for transfers between devices: 86.2 us -> 0.01 us  [local(): key_rows = lax.all_gather(own_keys, ('row', 'col'), axis=0, tiled=True)]
    unnamed x77 -> x82, local copies, waits for them, and re-layouts: 106 us -> 73.5 us
    reshape x0 -> x1, local copies, waits for them, and re-layouts: none -> 31.2 us  [local(): jnp.concatenate(lax.all_to_all(jnp.stack([own_values] * lax.axis_size(('r...]
    all_gather x1 -> x0, waiting for transfers between devices: 22.9 us -> none  [local(): lax.all_gather(own_values, ('row', 'col'), axis=0, tiled=True)]
    ppermute x4, starting transfers between devices: 10 us -> 32.9 us  [with_halo(): lax.ppermute(lax.slice_in_dim(block, block.shape[dim] - width, None, axis...]
    all_to_all x0 -> x1, starting transfers between devices: none -> 11.2 us  [local(): lax.all_to_all(jnp.stack([own_values] * lax.axis_size(('row', 'col'))), (...]
    another operation x0 -> x1, local copies, waits for them, and re-layouts: none -> 8.76 us  [local(): jnp.stack([own_values] * lax.axis_size(('row', 'col')))]
  transfers between devices with their start and end apart: 10 -> 10, of which waited for: 4 -> 3; matrix products, arithmetic and copies ran while one was open for 26% -> 9% of each run, Pallas kernels for 0% -> 0%
where the time goes in v1:
time: 711 us; the launch traced here: 705 us
  waiting for transfers between devices  395 us (56%)
  local copies, waits for them, and re-layouts  139 us (20%)
  matrix products  67.5 us (9%)
  starting transfers between devices  55.6 us (8%)
  other arithmetic  27.4 us (4%)
  between operations  20.6 us (3%)
    all_to_all x1, waiting for transfers between devices, local(): lax.all_to_all(jnp.stack([own_values] * lax.axis_size(('row', 'col'))), (...  390 us
    unnamed x82, local copies, waits for them, and re-layouts  73.5 us
    ppermute x4, starting transfers between devices, with_halo(): lax.ppermute(lax.slice_in_dim(block, block.shape[dim] - width, None, axis...  32.9 us
    reshape x1, local copies, waits for them, and re-layouts, local(): jnp.concatenate(lax.all_to_all(jnp.stack([own_values] * lax.axis_size(('r...  31.2 us
    dot_general x1, matrix products, local(): jnp.einsum('qc,kc->qk', queries, key_rows, preferred_element_type=jnp.flo...  24.6 us
    dot_general x1, matrix products, local(): jnp.dot(expos.astype(jnp.bfloat16), jnp.concatenate(lax.all_to_all(jnp.st...  22 us
    dot_general x2, matrix products, convolve(): jnp.dot(stacked, kernel.reshape(27 * channels, kernel.shape[-1]), preferr...  17.3 us
    reduce_sum x1, other arithmetic, local(): denominator = jnp.sum(expos, axis=1)  15.2 us
  transfers between devices with their start and end apart: 10, of which 3 were waited for; matrix products, arithmetic and copies ran while one was open for 9% of the time, Pallas kernels for 0%

profile of v1, /device:TPU:3, one launch (start us, length us, event | category | flops | bytes accessed | tf_op | source)
XLA Modules:
  0.0 704.7 jit_solution(5974541317709002844)
XLA Ops:
  8.8 1.9 fusion.15
  12.0 8.8 %stack.2 = bf16[128,260,384]{2,1,0:T(8,128)(2,1)} broadcast(bf16[260,384]{1,0:T(8,128)(2,1)S(1)} %convolution_convert_fusion.1), dimensions={1,2} | broadcast | bytes 25758720 | tf_op jit(solution)/shard_map/stack | solution.py:127
  20.8 11.2 %all-to-all-start = ((bf16[128,260,384]{2,1,0:T(8,128)(2,1)}), bf16[128,260,384]{2,1,0:T(8,128)(2,1)}, u32[]{:S(2)}, u32[]{:S(2)}) async-start(bf16[128,260,384]{2,1,0:T(8,128)(2,1)} %stack.2), calls=%async_computation | async-start | bytes 51904512 | tf_op jit(solution)/shard_map/all_to_all | solution.py:126
  37.5 389.8 %all-to-all-done = bf16[128,260,384]{2,1,0:T(8,128)(2,1)} async-done(((bf16[128,260,384]{2,1,0:T(8,128)(2,1)}), bf16[128,260,384]{2,1,0:T(8,128)(2,1)}, u32[]{:S(2)}, u32[]{:S(2)}) %all-to-all-start) | async-done | bytes 25559072 | tf_op jit(solution)/shard_map/all_to_all | solution.py:126
  427.3 31.2 %reshape.389 = bf16[33280,384]{1,0:T(8,128)(2,1)} reshape(bf16[128,260,384]{2,1,0:T(8,128)(2,1)} %all-to-all-done) | data formatting | bytes 51118080 | tf_op jit(solution)/shard_map/reshape | solution.py:125
  458.6 31.2 %reshape.394 = bf16[33280,384]{1,0:T(8,128)(2,1)} reshape(bf16[128,260,384]{2,1,0:T(8,128)(2,1)} %all-gather.3.cloned.1.call-done) | data formatting | bytes 51118080
  489.8 24.6 %fusion.98 = (f32[260]{0:T(512)S(1)}, f32[260,33280]{1,0:T(8,128)}) fusion(bf16[33280,384]{1,0:T(8,128)(2,1)} %reshape.394, bf16[260,384]{1,0:T(8,128)(2,1)S(1)} %reshape.388, bf16[384,384]{1,0:T(8,128)(2,1)S(1)} %copy-done, pred[33280]{0:T(1024)(128)(4,1)S(1)} %get-tuple-element.6), kind=kOutput, calls=%fused_computation.207 | convolution fusion | flops 6748085248 | bytes 60699152 | tf_op jit(solution)/shard_map/qc,kc->qk/dot_general | solution.py:118
  514.4 15.2 %fusion.1 = f32[260]{0:T(512)S(1)} fusion(f32[260,33280]{1,0:T(8,128)} %get-tuple-element.16, f32[33280]{0:T(1024)S(1)} %get-tuple-element.5, f32[260]{0:T(512)S(1)} %broadcast_maximum_fusion), kind=kLoop, calls=%fused_computation.3 | loop fusion | flops 25958140 | bytes 34746400 | tf_op jit(solution)/shard_map/reduce_sum | solution.py:122
  529.6 22.0 %fusion.12 = bf16[260,384]{1,0:T(8,128)(2,1)S(1)} fusion(bf16[33280,384]{1,0:T(8,128)(2,1)} %reshape.389, f32[260,33280]{1,0:T(8,128)} %get-tuple-element.16, f32[33280]{0:T(1024)S(1)} %get-tuple-element.5, f32[260]{0:T(512)S(1)} %broadcast_maximum_fusion, f32[260]{0:T(512)S(1)} %fusion.1), kind=kOutput, calls=%fused_computation.19 | convolution fusion | flops 6671508480 | bytes 60505120 | tf_op jit(solution)/shard_map/dot_general | solution.py:123
  552.6 1.5 dynamic_update_slice.25
  554.2 22.3 %collective-permute-start = (bf16[3,1,20,384]{3,2,1,0:T(8,128)(2,1)S(1)}, bf16[3,1,20,384]{3,2,1,0:T(8,128)(2,1)S(1)}, u32[]{:S(2)}, u32[]{:S(2)}) collective-permute-start(bf16[3,1,20,384]{3,2,1,0:T(8,128)(2,1)S(1)} %get-tuple-element.13), channel_id=1, source_target_pairs={{0,16},{16,32},{32,48},{48,64},{64,80},{80,96},{96,112},{1,17},{17... | collective-permute-start | bytes 138248 | tf_op jit(solution)/shard_map/ppermute | solution.py:16
  576.6 2.1 collective-permute-start.1
  578.7 1.6 constant_dynamic-update-slice_fusion.1
  582.2 1.9 collective-permute-start.2
  584.1 5.5 collective-permute-start.3
  592.8 1.7 pad_maximum_fusion.2
  594.6 1.8 dynamic_update_slice.27
  598.3 6.2 multiply_reduce_fusion
  607.8 3.4 dynamic_update_slice.29
  611.3 3.1 collective-permute-start.4
  614.4 1.9 collective-permute-start.5
  616.4 3.9 collective-permute-done.5
  620.5 5.6 collective-permute-start.6
  626.1 1.9 collective-permute-start.7
  628.1 7.9 %copy.21 = bf16[3,3,3,384,192]{3,2,1,0,4:T(4,128)(2,1)} copy(bf16[3,3,3,384,192]{3,4,2,1,0:T(8,128)(2,1)} %param.27) | data formatting | bytes 7962624 | tf_op args[13]
  635.9 10.1 %reshape.396 = bf16[10368,192,1]{0,1,2:T(8,128)(2,1)} reshape(bf16[3,3,3,384,192]{3,2,1,0,4:T(4,128)(2,1)} %copy.21) | data formatting | bytes 7962624 | tf_op jit(solution)/shard_map/reshape | solution.py:67
  646.7 4.4 pad_maximum_fusion
  651.3 3.6 dynamic_update_slice.31
  670.1 1.3 fusion.29
  673.7 1.3 fusion.26
  678.5 1.3 fusion.22
  686.7 11.2 %fusion.7 = bf16[26,40,192]{2,1,0:T(8,128)(2,1)} fusion(bf16[26,40,10368]{2,1,0:T(8,128)(2,1)} %fusion.16, bf16[10368,192,1]{0,1,2:T(8,128)(2,1)S(1)} %copy-done.4, pred[26,40]{1,0:T(8,128)(4,1)S(1)} %broadcast_and_fusion), kind=kOutput, calls=%fused_computation.12 | convolution fusion | flops 4140963840 | bytes 25947152 | tf_op jit(solution)/shard_map/dot_general | solution.py:66
  (131 shorter events, 42.7 us)
Async XLA Ops:
  6.5 483.2 %copy-start = (bf16[384,384]{1,0:T(8,128)(2,1)S(1)}, bf16[384,384]{1,0:T(8,128)(2,1)}, u32[]{:S(2)}) copy-start(bf16[384,384]{1,0:T(8,128)(2,1)} %param.18) | copy-start | bytes 884740
  6.5 452.0 %all-gather.3.cloned.1.call-start = ((), (), s32[]{:S(2)}) async-start(), calls=%async_computation.1 | async-start | bytes 26155008 | tf_op jit(solution)/shard_map/all_gather | solution.py:108
  20.8 11.3 %copy-start.6 = (bf16[2,13,20,384]{3,0,2,1:T(2,128)(2,1)S(1)}, bf16[2,13,20,384]{3,0,2,1:T(2,128)(2,1)}, u32[]{:S(2)}) copy-start(bf16[2,13,20,384]{3,0,2,1:T(2,128)(2,1)} %param.22) | copy-start | bytes 1198084
  20.8 11.3 %copy-start.11 = (s32[8]{0:T(128)S(1)}, s32[8]{0:T(128)}, u32[]{:S(2)}) copy-start(s32[8]{0:T(128)} %param.15) | copy-start | bytes 100
  20.8 13.4 %copy-start.12 = (s32[16]{0:T(128)S(1)}, s32[16]{0:T(128)}, u32[]{:S(2)}) copy-start(s32[16]{0:T(128)} %param.16) | copy-start | bytes 196
  20.8 406.5 %all-to-all-start = ((bf16[128,260,384]{2,1,0:T(8,128)(2,1)}), bf16[128,260,384]{2,1,0:T(8,128)(2,1)}, u32[]{:S(2)}, u32[]{:S(2)}) async-start(bf16[128,260,384]{2,1,0:T(8,128)(2,1)} %stack.2), calls=%async_computation | async-start | bytes 51904512 | tf_op jit(solution)/shard_map/all_to_all | solution.py:126
  529.6 22.1 %copy-start.7 = (bf16[384,384]{1,0:T(8,128)(2,1)S(1)}, bf16[384,384]{1,0:T(8,128)(2,1)}, u32[]{:S(2)}) copy-start(bf16[384,384]{1,0:T(8,128)(2,1)} %param.21) | copy-start | bytes 884740
  529.6 22.4 %copy-start.5 = (bf16[13,20,384]{2,1,0:T(8,128)(2,1)S(1)}, bf16[13,20,384]{2,1,0:T(8,128)(2,1)}, u32[]{:S(2)}) copy-start(bf16[13,20,384]{2,1,0:T(8,128)(2,1)} %param.14) | copy-start | bytes 599044
  529.6 22.6 %copy-start.9 = (f32[384]{0:T(512)S(1)}, f32[384]{0:T(512)}, u32[]{:S(2)}) copy-start(f32[384]{0:T(512)} %param.23) | copy-start | bytes 4612
  554.2 38.6 %copy-start.3 = (bf16[3,13,20,384]{3,2,1,0:T(8,128)(2,1)}, bf16[3,13,20,384]{3,2,1,0:T(8,128)(2,1)S(1)}, u32[]{:S(2)}) copy-start(bf16[3,13,20,384]{3,2,1,0:T(8,128)(2,1)S(1)} %dynamic_update_slice.25) | copy-start | bytes 1797124
  554.2 26.7 %collective-permute-start = (bf16[3,1,20,384]{3,2,1,0:T(8,128)(2,1)S(1)}, bf16[3,1,20,384]{3,2,1,0:T(8,128)(2,1)S(1)}, u32[]{:S(2)}, u32[]{:S(2)}) collective-permute-start(bf16[3,1,20,384]{3,2,1,0:T(8,128)(2,1)S(1)} %get-tuple-element.13), channel_id=1, source_target_pairs={{0,16},{16,32},{32,48},{48,64},{64,80},{80,96},{96,112},{1,17},{17... | collective-permute-start | bytes 138248 | tf_op jit(solution)/shard_map/ppermute | solution.py:16
  576.6 5.5 collective-permute-start.1
  582.2 10.7 %collective-permute-start.2 = (bf16[3,15,1,384]{3,2,1,0:T(2,128)(2,1)S(1)}, bf16[3,15,1,384]{3,2,1,0:T(2,128)(2,1)S(1)}, u32[]{:S(2)}, u32[]{:S(2)}) collective-permute-start(bf16[3,15,1,384]{3,2,1,0:T(2,128)(2,1)S(1)} %get-tuple-element.11), channel_id=1, source_target_pairs={{0,1},{1,2},{2,3},{3,4},{4,5},{5,6},{6,7},{7,8},{8,9},{9,10},{10,1... | collective-permute-start | bytes 103688 | tf_op jit(solution)/shard_map/ppermute | solution.py:16
  584.1 8.7 %collective-permute-start.3 = (bf16[3,15,1,384]{3,2,1,0:T(2,128)(2,1)S(1)}, bf16[3,15,1,384]{3,2,1,0:T(2,128)(2,1)}, u32[]{:S(2)}, u32[]{:S(2)}) collective-permute-start(bf16[3,15,1,384]{3,2,1,0:T(2,128)(2,1)S(1)} %get-tuple-element.12), channel_id=1, source_target_pairs={{1,0},{2,1},{3,2},{4,3},{5,4},{6,5},{7,6},{8,7},{9,8},{10,9},{11,1... | collective-permute-start | bytes 103688 | tf_op jit(solution)/shard_map/ppermute | solution.py:19
  598.3 6.2 copy-start.10
  611.3 34.8 %copy-start.2 = (bf16[3,26,40,384]{3,2,1,0:T(8,128)(2,1)}, bf16[3,26,40,384]{3,2,1,0:T(8,128)(2,1)S(1)}, u32[]{:S(2)}) copy-start(bf16[3,26,40,384]{3,2,1,0:T(8,128)(2,1)S(1)} %dynamic_update_slice.29) | copy-start | bytes 7188484
  611.3 5.1 collective-permute-start.4
  614.4 5.9 collective-permute-start.5
  620.5 25.5 %collective-permute-start.6 = (bf16[3,28,1,384]{3,2,1,0:T(2,128)(2,1)S(1)}, bf16[3,28,1,384]{3,2,1,0:T(2,128)(2,1)S(1)}, u32[]{:S(2)}, u32[]{:S(2)}) collective-permute-start(bf16[3,28,1,384]{3,2,1,0:T(2,128)(2,1)S(1)} %get-tuple-element.7), channel_id=1, source_target_pairs={{0,1},{1,2},{2,3},{3,4},{4,5},{5,6},{6,7},{7,8},{8,9},{9,10},{10,1... | collective-permute-start | bytes 193544 | tf_op jit(solution)/shard_map/ppermute | solution.py:16
  626.1 20.6 %collective-permute-start.7 = (bf16[3,28,1,384]{3,2,1,0:T(2,128)(2,1)S(1)}, bf16[3,28,1,384]{3,2,1,0:T(2,128)(2,1)}, u32[]{:S(2)}, u32[]{:S(2)}) collective-permute-start(bf16[3,28,1,384]{3,2,1,0:T(2,128)(2,1)S(1)} %get-tuple-element.8), channel_id=1, source_target_pairs={{1,0},{2,1},{3,2},{4,3},{5,4},{6,5},{7,6},{8,7},{9,8},{10,9},{11,1... | collective-permute-start | bytes 193544 | tf_op jit(solution)/shard_map/ppermute | solution.py:19
  646.0 0.7 copy-start.8
  677.3 9.4 %copy-start.4 = (bf16[10368,192,1]{0,1,2:T(8,128)(2,1)S(1)}, bf16[10368,192,1]{0,1,2:T(8,128)(2,1)}, u32[]{:S(2)}) copy-start(bf16[10368,192,1]{0,1,2:T(8,128)(2,1)} %reshape.396) | copy-start | bytes 11943940
  686.7 11.2 %copy-start.1 = (bf16[384,384]{1,0:T(8,128)(2,1)S(1)}, bf16[384,384]{1,0:T(8,128)(2,1)}, u32[]{:S(2)}) copy-start(bf16[384,384]{1,0:T(8,128)(2,1)} %param.18) | copy-start | bytes 884740
Sparse Core Ops, SparseCore 0:
  10.9 366.1 all-gather.2
